TPU v7x, 32 devices: a whole 2x2x4 slice. The times are simulated.
32 devices in a mesh: row: 4 (over y, x), dict: 8 (over z, core).
Axes of the slice: x: 2, y: 2, z: 4, core: 2. Of those that a mesh axis runs over, the one named last changes fastest.
Arguments:
- activations: bfloat16 [4096, 4096], P(('row', 'dict')), may hold values from -6 to 6
- block_ids: int32 [4096, 4], P(('row', 'dict')), may hold values from 0 to 15, all different within a row; in each aligned block of 128 rows (0 to 127, 128 to 255, ...) at most 48 rows name the same one
- enc_weight: bfloat16 [2048, 4096], P('dict'), may hold values from -0.09375 to 0.09375
- enc_bias: float32 [2048], P('dict'), may hold values from -3 to 3
- dec_weight: bfloat16 [2048, 4096], P('dict'), may hold values from -0.25 to 0.25
- dec_bias: float32 [4096], replicated, may hold values from -3 to 3
Outputs:
- rebuilt: bfloat16 [4096, 4096], P(('row', 'dict'))
- enc_grad: bfloat16 [4096, 2048], P('row', 'dict')
- dec_grad: bfloat16 [4096, 2048], P('row', 'dict')
Inputs may be any that keep to these rules, and one draw needn't show every extreme that they name: `block_ids`: each row names 4 different blocks. Among the rows of one device no block is named by more than 48 rows, and some block is named by exactly 48.
All inputs are finite; a program needn't handle non-finite values.
Results may differ from a plain program's by a relative error of at most 0.0059.
Values may be sent and summed in bfloat16 or wider, within the bound.
A program may use at most 128 MiB of HBM per device.

v0:
```python
import jax
import jax.numpy as jnp
from jax import lax
from jax.sharding import PartitionSpec as P

BS = 128
K = 4
LOSS_SCALE = 0.03125


def gelu_tanh(values):
    return jax.nn.gelu(values, approximate=True)


def gelu_grad(pre_act, upstream):
    return jax.vjp(gelu_tanh, pre_act)[1](upstream)[0]


def slot_plan(block_ids, groups, total_blocks, slot_depth):
    rows_total = block_ids.shape[0]
    picks = block_ids.shape[1]
    per_group = rows_total // groups
    flat_ids = block_ids.reshape(groups, per_group * picks)
    onehot = (
        flat_ids[:, :, None] == jnp.arange(total_blocks, dtype=jnp.int32)[None, None, :]
    ).astype(jnp.int32)
    rank_in_block = jnp.sum((jnp.cumsum(onehot, axis=1) - 1) * onehot, axis=2)
    group_index = jnp.arange(groups, dtype=jnp.int32)[:, None]
    target = ((flat_ids * groups + group_index) * slot_depth + rank_in_block).reshape(-1)
    source_row = jnp.arange(rows_total * picks, dtype=jnp.int32) // picks
    filled = (
        jnp.full((total_blocks * groups * slot_depth,), rows_total, jnp.int32)
        .at[target]
        .set(source_row)
    )
    return (target, filled)


def pack_rows(values, filled, shape):
    padded = jnp.concatenate([values, jnp.zeros((1, values.shape[1]), values.dtype)], axis=0)
    return padded[filled].reshape(shape)


def on_device(activations, block_ids, enc_weight, enc_bias, dec_weight, dec_bias):
    rows_here, features = activations.shape
    dict_size = lax.axis_size("dict")
    row_size = lax.axis_size("row")
    local_latents = enc_weight.shape[0]
    block_count = local_latents // BS
    total_blocks = block_count * dict_size
    slot_depth = max(2, 3 * rows_here * K // (2 * total_blocks))
    enc_blocks = enc_weight.reshape(block_count, BS, features)
    dec_blocks = dec_weight.reshape(block_count, BS, features)
    bias_blocks = enc_bias.reshape(block_count, BS)
    shifted = (activations.astype(jnp.float32) - dec_bias[None, :]).astype(jnp.bfloat16)
    target, filled = slot_plan(block_ids, 1, total_blocks, slot_depth)
    outgoing = pack_rows(shifted, filled, (dict_size, block_count, slot_depth, features))
    encode_received = lax.all_to_all(outgoing, "dict", split_axis=0, concat_axis=0, tiled=True)
    pre_act = jnp.einsum(
        "sbmd,bcd->sbmc", encode_received, enc_blocks, preferred_element_type=jnp.float32
    )
    pre_act = pre_act + bias_blocks[None, :, None, :]
    encode_latent = gelu_tanh(pre_act).astype(jnp.bfloat16)
    partial_value = jnp.einsum(
        "sbmc,bcd->sbmd", encode_latent, dec_blocks, preferred_element_type=jnp.float32
    ).astype(jnp.bfloat16)
    partial_value, pre_act, latent, received = (
        partial_value,
        pre_act,
        encode_latent,
        encode_received,
    )
    returned = lax.all_to_all(partial_value, "dict", split_axis=0, concat_axis=0, tiled=True)
    slot_parts = (
        returned.reshape(-1, features)[target].astype(jnp.float32).reshape(rows_here, K, features)
    )
    recon_full = dec_bias[None, :] + jnp.sum(slot_parts, axis=1)
    rebuilt = recon_full.astype(jnp.bfloat16)
    residual = ((recon_full - activations.astype(jnp.float32)) * LOSS_SCALE).astype(jnp.bfloat16)
    residual_sent = pack_rows(residual, filled, (dict_size, block_count, slot_depth, features))
    residual_held = lax.all_to_all(residual_sent, "dict", split_axis=0, concat_axis=0, tiled=True)
    upstream = jnp.einsum(
        "sbmd,bcd->sbmc", residual_held, dec_blocks, preferred_element_type=jnp.float32
    )
    latent_grad = gelu_grad(pre_act, upstream).astype(jnp.bfloat16)
    product = jnp.einsum(
        "sbmc,sbmd->dbc", latent, residual_held, preferred_element_type=jnp.float32
    )
    dec_grad = lax.psum_scatter(
        product.reshape(features // row_size * lax.axis_size("row"), local_latents),
        "row",
        scatter_dimension=0,
        tiled=True,
    ).astype(jnp.bfloat16)
    product = jnp.einsum(
        "sbmc,sbmd->dbc", latent_grad, received, preferred_element_type=jnp.float32
    )
    enc_grad = lax.psum_scatter(
        product.reshape(features // row_size * lax.axis_size("row"), local_latents),
        "row",
        scatter_dimension=0,
        tiled=True,
    ).astype(jnp.bfloat16)
    return (rebuilt, enc_grad, dec_grad)


def gelu_and_slope(values):
    inner = 0.7978845608 * (values + 0.044715 * values * values * values)
    bend = jnp.tanh(inner)
    half = 0.5 * (1.0 + bend)
    slope = half + 0.5 * values * (1.0 - bend * bend) * 0.7978845608 * (
        1.0 + 3.0 * 0.044715 * values * values
    )
    return (values * half, slope)


def dense_on_device(activations, block_ids, enc_weight, enc_bias, dec_weight, dec_bias):
    local_latents = enc_weight.shape[0]
    block_count = local_latents // BS
    me = lax.axis_index("dict")
    shifted = (activations.astype(jnp.float32) - dec_bias[None, :]).astype(jnp.bfloat16)
    ids = lax.all_gather(block_ids, "dict", axis=0, tiled=True)
    held = lax.all_gather(shifted, "dict", axis=0, tiled=True)
    mine = me * block_count + jnp.arange(local_latents, dtype=jnp.int32) // BS
    mask = jnp.any(ids[:, :, None] == mine[None, None, :], axis=1)
    pre_act = lax.dot_general(
        held, enc_weight, (((1,), (1,)), ((), ())), preferred_element_type=jnp.float32
    )
    pre_act = pre_act + enc_bias[None, :]
    value, slope = gelu_and_slope(pre_act)
    latent = jnp.where(mask, value, 0.0).astype(jnp.bfloat16)
    slope = jnp.where(mask, slope, 0.0)
    partial_sum = jnp.dot(latent, dec_weight, preferred_element_type=jnp.float32)
    total = lax.psum_scatter(
        partial_sum.astype(jnp.bfloat16), "dict", scatter_dimension=0, tiled=True
    )
    recon_full = dec_bias[None, :] + total.astype(jnp.float32)
    rebuilt = recon_full.astype(jnp.bfloat16)
    residual = ((recon_full - activations.astype(jnp.float32)) * LOSS_SCALE).astype(jnp.bfloat16)
    residual_held = lax.all_gather(residual, "dict", axis=0, tiled=True)
    upstream = lax.dot_general(
        residual_held, dec_weight, (((1,), (1,)), ((), ())), preferred_element_type=jnp.float32
    )
    latent_grad = (slope * upstream).astype(jnp.bfloat16)

    def reduced(rows_by_features, rows_by_latents):
        product = lax.dot_general(
            rows_by_features,
            rows_by_latents,
            (((0,), (0,)), ((), ())),
            preferred_element_type=jnp.float32,
        )
        return lax.psum_scatter(product, "row", scatter_dimension=0, tiled=True).astype(
            jnp.bfloat16
        )

    dec_grad = reduced(residual_held, latent)
    enc_grad = reduced(held, latent_grad)
    return (rebuilt, enc_grad, dec_grad)


def solution(mesh):
    few_blocks = mesh.shape["dict"] <= 8
    return jax.shard_map(
        dense_on_device if few_blocks else on_device,
        mesh=mesh,
        in_specs=(
            P(("row", "dict"), None),
            P(("row", "dict"), None),
            P("dict", None),
            P("dict"),
            P("dict", None),
            P(),
        ),
        out_specs=(P(("row", "dict"), None), P("row", "dict"), P("row", "dict")),
        check_vma=False,
    )
```

profile of v0, /device:TPU:0, one launch (start us, length us, event | category | flops | bytes accessed | tf_op | source)
XLA Modules:
  0.0 404.1 jit_solution(12838851521415117076)
XLA Ops:
  7.2 0.0 copy-start
  7.2 0.0 all-gather.3.cloned.1.call-start
  7.2 2.5 fusion
  9.8 0.0 all-gather.3.cloned.1.call-update
  9.8 0.0 reduce-scatter.4.cloned.1.call-start
  9.8 14.5 %all_gather.9 = s32[1024,4]{0,1:T(4,128)S(1)} all-gather(s32[128,4]{0,1:T(4,128)} %param.7), channel_id=1, replica_groups=mesh['row'=4,'dict'=8] {'dict'}, dimensions={0}, use_global_device_ids=true | all-gather | bytes 18432 | tf_op jit(solution)/shard_map/all_gather | solution.py:122
  24.4 1.0 compare_reduce_fusion
  25.4 69.6 %all-gather.3.cloned.1.call-done = bf16[1024,4096]{1,0:T(8,128)(2,1)} async-done(((bf16[128,4096]{1,0:T(8,128)(2,1)}), bf16[1024,4096]{1,0:T(8,128)(2,1)}) %all-gather.3.cloned.1.call-update) | async-done | bytes 8388624 | tf_op jit(solution)/shard_map/all_gather | solution.py:123
  95.0 6.4 %convolution_add_fusion = f32[1024,256]{1,0:T(8,128)S(1)} fusion(bf16[1024,4096]{1,0:T(8,128)(2,1)} %all-gather.3.cloned.1.call-done, bf16[256,4096]{1,0:T(8,128)(2,1)} %param.8, f32[256]{0:T(256)} %param.9), kind=kOutput, calls=%fused_computation.12 | convolution fusion | flops 2147745792 | bytes 11535360 | tf_op jit(solution)/shard_map/dot_general | solution.py:126
  101.4 0.0 copy-start.2
  101.4 1.0 copy-done.2
  102.3 0.0 copy-done
  102.3 5.8 %convolution_convert_fusion = bf16[1024,4096]{1,0:T(8,128)(2,1)} fusion(bf16[256,4096]{1,0:T(8,128)(2,1)S(1)} %copy-done, pred[1024,256]{1,0:T(8,128)(4,1)S(1)} %compare_reduce_fusion, f32[1024,256]{1,0:T(8,128)S(1)} %convolution_add_fusion), kind=kOutput, calls=%fused_computation | convolution fusion | flops 2154299392 | bytes 11796480 | tf_op jit(solution)/shard_map/dot_general | solution.py:133
  108.1 0.0 reduce-scatter.4.cloned.1.call-update
  108.1 0.0 all-gather.5.cloned.1.call-start
  108.2 88.3 %reduce-scatter.4.cloned.1.call-done = bf16[128,4096]{1,0:T(8,128)(2,1)} async-done(((bf16[1024,4096]{1,0:T(8,128)(2,1)}), bf16[128,4096]{1,0:T(8,128)(2,1)}) %reduce-scatter.4.cloned.1.call-update) | async-done | bytes 1048592 | tf_op jit(solution)/shard_map/reduce_scatter | solution.py:134
  196.4 0.0 copy-done.1
  196.4 0.0 copy-done.4
  196.4 3.0 fusion.2
  199.5 0.0 all-gather.5.cloned.1.call-update
  199.5 0.0 reduce-scatter.8.cloned.1.call-start
  199.5 80.5 %all-gather.5.cloned.1.call-done = bf16[1024,4096]{1,0:T(8,128)(2,1)} async-done(((bf16[128,4096]{1,0:T(8,128)(2,1)}), bf16[1024,4096]{1,0:T(8,128)(2,1)}) %all-gather.5.cloned.1.call-update) | async-done | bytes 8388624 | tf_op jit(solution)/shard_map/all_gather | solution.py:140
  280.1 8.2 %fusion.12 = f32[4096,256]{1,0:T(8,128)} fusion(bf16[1024,4096]{1,0:T(8,128)(2,1)} %all-gather.5.cloned.1.call-done, pred[1024,256]{1,0:T(8,128)(4,1)S(1)} %compare_reduce_fusion, f32[1024,256]{1,0:T(8,128)} %copy-done.2), kind=kOutput, calls=%fused_computation.27 | convolution fusion | flops 2150105088 | bytes 13893632 | tf_op jit(solution)/shard_map/dot_general | solution.py:147
  288.2 0.0 reduce-scatter.8.cloned.1.call-update
  288.3 0.2 reduce-scatter.6.cloned.1.call-start
  288.5 1.0 copy-done.3
  289.5 17.6 %fusion.13 = f32[4096,256]{1,0:T(8,128)} fusion(bf16[1024,4096]{1,0:T(8,128)(2,1)} %all-gather.3.cloned.1.call-done, bf16[1024,4096]{1,0:T(8,128)(2,1)} %all-gather.5.cloned.1.call-done, bf16[256,4096]{1,0:T(8,128)(2,1)S(1)} %copy-done, pred[1024,256]{1,0:T(8,128)(4,1)S(1)} %compare_reduce_fusion, f32[1024,256]{1,0:T(8,128)S(1)} %copy-done.3), kind=kOutput, calls=%fused_computation.28 | convolution fusion | flops 4300210176 | bytes 24379392 | tf_op jit(solution)/shard_map/dot_general | solution.py:147
  307.1 0.0 reduce-scatter.6.cloned.1.call-update
  307.1 32.5 %reduce-scatter.8.cloned.1.call-done = f32[1024,256]{1,0:T(8,128)} async-done(((f32[4096,256]{1,0:T(8,128)}), f32[1024,256]{1,0:T(8,128)}) %reduce-scatter.8.cloned.1.call-update) | async-done | bytes 1048592 | tf_op jit(solution)/shard_map/reduce_scatter | solution.py:153
  339.6 2.1 convert_element_type.40
  341.7 53.8 %reduce-scatter.6.cloned.1.call-done = f32[1024,256]{1,0:T(8,128)} async-done(((f32[4096,256]{1,0:T(8,128)}), f32[1024,256]{1,0:T(8,128)}) %reduce-scatter.6.cloned.1.call-update) | async-done | bytes 1048592 | tf_op jit(solution)/shard_map/reduce_scatter | solution.py:153
  395.5 2.1 convert_element_type.39
  (4 shorter events, 0.0 us)
Async XLA Ops:
  7.2 95.2 %copy-start = (bf16[256,4096]{1,0:T(8,128)(2,1)S(1)}, bf16[256,4096]{1,0:T(8,128)(2,1)}, u32[]{:S(2)}) copy-start(bf16[256,4096]{1,0:T(8,128)(2,1)} %param.10) | copy-start | bytes 6291460
  7.2 87.8 %all-gather.3.cloned.1.call-start = ((), (), s32[]{:S(2)}) async-start(), calls=%async_computation.3 | async-start | bytes 9437184 | tf_op jit(solution)/shard_map/all_gather | solution.py:123
  9.8 186.6 %reduce-scatter.4.cloned.1.call-start = ((), (), s32[]{:S(2)}) async-start(), calls=%async_computation.4 | async-start | bytes 9437184 | tf_op jit(solution)/shard_map/reduce_scatter | solution.py:134
  101.4 1.0 copy-start.2
  108.1 88.3 %copy-start.1 = (bf16[128,4096]{1,0:T(8,128)(2,1)S(1)}, bf16[128,4096]{1,0:T(8,128)(2,1)}, u32[]{:S(2)}) copy-start(bf16[128,4096]{1,0:T(8,128)(2,1)} %param.6) | copy-start | bytes 3145732
  108.1 88.3 %copy-start.4 = (f32[4096]{0:T(1024)S(1)}, f32[4096]{0:T(1024)}, u32[]{:S(2)}) copy-start(f32[4096]{0:T(1024)} %param.11) | copy-start | bytes 49156
  108.1 171.9 %all-gather.5.cloned.1.call-start = ((), (), s32[]{:S(2)}) async-start(), calls=%async_computation.5 | async-start | bytes 9437184 | tf_op jit(solution)/shard_map/all_gather | solution.py:140
  199.5 140.1 %reduce-scatter.8.cloned.1.call-start = ((), (), s32[]{:S(2)}) async-start(), calls=%async_computation.7 | async-start | bytes 5242880 | tf_op jit(solution)/shard_map/reduce_scatter | solution.py:153
  288.2 1.2 copy-start.3
  288.3 107.2 %reduce-scatter.6.cloned.1.call-start = ((), (), s32[]{:S(2)}) async-start(), calls=%async_computation.6 | async-start | bytes 5242880 | tf_op jit(solution)/shard_map/reduce_scatter | solution.py:153
Sparse Core Ops, SparseCore 0:
  10.2 84.7 all-gather.2
  108.2 88.1 reduce-scatter.3
  199.6 80.3 all-gather.4
  288.4 51.2 reduce-scatter.7
  342.7 52.6 reduce-scatter.5
where the time goes:
time: 404 us
  waiting for transfers between devices  325 us (80%)
  matrix products  38 us (9%)
  blocking collectives  14.5 us (4%)
  between operations  13.8 us (3%)
  other arithmetic  10.7 us (3%)
    reduce_scatter x1, waiting for transfers between devices, dense_on_device(): lax.psum_scatter(partial_sum.astype(jnp.bfloat16), 'dict', scatter_dimens...  88.3 us
    reduce_scatter x2, waiting for transfers between devices, reduced(): lax.psum_scatter(product, 'row', scatter_dimension=0, tiled=True)  86.3 us
    all_gather x1, waiting for transfers between devices, dense_on_device(): residual_held = lax.all_gather(residual, 'dict', axis=0, tiled=True)  80.5 us
    all_gather x1, waiting for transfers between devices, dense_on_device(): held = lax.all_gather(shifted, 'dict', axis=0, tiled=True)  69.6 us
    dot_general x2, matrix products, reduced(): lax.dot_general(rows_by_features, rows_by_latents, (((0,), (0,)), ((), ()...  25.8 us
    all_gather x1, blocking collectives, dense_on_device(): ids = lax.all_gather(block_ids, 'dict', axis=0, tiled=True)  14.5 us
  transfers between devices with their start and end apart: 5, of which 5 were waited for; matrix products, arithmetic and copies ran while one was open for 5% of the time, Pallas kernels for 0%

commit v1 on v0

--- a/solution.py
+++ b/solution.py
@@ -119,8 +119,11 @@
     block_count = local_latents // BS
     me = lax.axis_index("dict")
     shifted = (activations.astype(jnp.float32) - dec_bias[None, :]).astype(jnp.bfloat16)
-    ids = lax.all_gather(block_ids, "dict", axis=0, tiled=True)
-    held = lax.all_gather(shifted, "dict", axis=0, tiled=True)
+    ids, held = jnp.split(
+        lax.all_gather(jnp.concatenate([block_ids, shifted], axis=1), "dict", axis=0, tiled=True),
+        [block_ids.shape[1]],
+        axis=1,
+    )
     mine = me * block_count + jnp.arange(local_latents, dtype=jnp.int32) // BS
     mask = jnp.any(ids[:, :, None] == mine[None, None, :], axis=1)
     pre_act = lax.dot_general(

time: 404 us -> 411 us (1.017)
  waiting for transfers between devices: 325 us -> 342 us
  blocking collectives: 14.5 us -> 0 us
    all_gather x1, waiting for transfers between devices: 69.6 us -> 87 us  [dense_on_device(): lax.all_gather(jnp.concatenate([block_ids, shifted], axis=1), 'dict', axi...]
    all_gather x1 -> x0, blocking collectives: 14.5 us -> none  [dense_on_device(): ids = lax.all_gather(block_ids, 'dict', axis=0, tiled=True)]
where the time goes in v1:
time: 411 us; the launch traced here: 410 us
  waiting for transfers between devices  342 us (83%)
  matrix products  39.2 us (10%)
  between operations  13.9 us (3%)
  other arithmetic  11.7 us (3%)
    reduce_scatter x1, waiting for transfers between devices, dense_on_device(): lax.psum_scatter(partial_sum.astype(jnp.bfloat16), 'dict', scatter_dimens...  88.2 us
    all_gather x1, waiting for transfers between devices, dense_on_device(): lax.all_gather(jnp.concatenate([block_ids, shifted], axis=1), 'dict', axi...  87 us
    reduce_scatter x2, waiting for transfers between devices, reduced(): lax.psum_scatter(product, 'row', scatter_dimension=0, tiled=True)  86.1 us
    all_gather x1, waiting for transfers between devices, dense_on_device(): residual_held = lax.all_gather(residual, 'dict', axis=0, tiled=True)  80.5 us
    dot_general x2, matrix products, reduced(): lax.dot_general(rows_by_features, rows_by_latents, (((0,), (0,)), ((), ()...  25.9 us
  transfers between devices with their start and end apart: 5, of which 5 were waited for; matrix products, arithmetic and copies ran while one was open for 5% of the time, Pallas kernels for 0%

profile of v1, /device:TPU:0, one launch (start us, length us, event | category | flops | bytes accessed | tf_op | source)
XLA Modules:
  0.0 410.3 jit_solution(8900284311634450629)
XLA Ops:
  7.2 0.0 copy-start
  7.2 0.0 all-gather.3.cloned.1.call-start
  7.2 0.8 convert_element_type.42
  8.1 0.1 copy.10
  8.2 1.4 fusion.4
  9.6 1.5 pad_maximum_fusion
  11.1 0.0 all-gather.3.cloned.1.call-update
  11.1 0.0 reduce-scatter.4.cloned.1.call-start
  11.2 87.0 %all-gather.3.cloned.1.call-done = bf16[1024,4100]{1,0:T(8,128)(2,1)} async-done(((bf16[128,4100]{1,0:T(8,128)(2,1)}), bf16[1024,4100]{1,0:T(8,128)(2,1)}) %all-gather.3.cloned.1.call-update) | async-done | bytes 8396816 | tf_op jit(solution)/shard_map/all_gather | solution.py:123
  98.2 1.0 split.8
  99.2 0.1 copy.11
  99.3 0.9 compare_reduce_fusion
  100.2 7.5 %fusion.8 = f32[1024,256]{1,0:T(8,128)S(1)} fusion(bf16[256,4096]{1,0:T(8,128)(2,1)} %param.8, bf16[1024,4100]{1,0:T(8,128)(2,1)} %all-gather.3.cloned.1.call-done, f32[256]{0:T(256)S(1)} %copy-done.5), kind=kOutput, calls=%fused_computation.16 | convolution fusion | flops 2147745792 | bytes 11535360 | tf_op jit(solution)/shard_map/dot_general | solution.py:129
  107.7 1.0 copy-done.2
  108.7 5.7 %convolution_convert_fusion = bf16[1024,4096]{1,0:T(8,128)(2,1)} fusion(bf16[256,4096]{1,0:T(8,128)(2,1)S(1)} %copy-done, pred[1024,256]{1,0:T(8,128)(4,1)S(1)} %compare_reduce_fusion, f32[1024,256]{1,0:T(8,128)S(1)} %fusion.8), kind=kOutput, calls=%fused_computation | convolution fusion | flops 2154299392 | bytes 11796480 | tf_op jit(solution)/shard_map/dot_general | solution.py:136
  114.5 0.0 reduce-scatter.4.cloned.1.call-update
  114.5 0.0 all-gather.5.cloned.1.call-start
  114.5 88.2 %reduce-scatter.4.cloned.1.call-done = bf16[128,4096]{1,0:T(8,128)(2,1)} async-done(((bf16[1024,4096]{1,0:T(8,128)(2,1)}), bf16[128,4096]{1,0:T(8,128)(2,1)}) %reduce-scatter.4.cloned.1.call-update) | async-done | bytes 1048592 | tf_op jit(solution)/shard_map/reduce_scatter | solution.py:137
  202.8 3.0 fusion.6
  205.8 0.0 all-gather.5.cloned.1.call-update
  205.8 0.0 reduce-scatter.8.cloned.1.call-start
  205.8 80.5 %all-gather.5.cloned.1.call-done = bf16[1024,4096]{1,0:T(8,128)(2,1)} async-done(((bf16[128,4096]{1,0:T(8,128)(2,1)}), bf16[1024,4096]{1,0:T(8,128)(2,1)}) %all-gather.5.cloned.1.call-update) | async-done | bytes 8388624 | tf_op jit(solution)/shard_map/all_gather | solution.py:143
  286.3 8.2 %fusion.20 = f32[4096,256]{1,0:T(8,128)} fusion(bf16[1024,4096]{1,0:T(8,128)(2,1)} %all-gather.5.cloned.1.call-done, pred[1024,256]{1,0:T(8,128)(4,1)S(1)} %compare_reduce_fusion, f32[1024,256]{1,0:T(8,128)} %copy-done.2), kind=kOutput, calls=%fused_computation.33 | convolution fusion | flops 2150105088 | bytes 13893632 | tf_op jit(solution)/shard_map/dot_general | solution.py:150
  294.5 0.0 reduce-scatter.8.cloned.1.call-update
  294.5 0.2 reduce-scatter.6.cloned.1.call-start
  294.8 1.0 copy-done.3
  295.7 17.8 %fusion = f32[4096,256]{1,0:T(8,128)} fusion(bf16[1024,4100]{1,0:T(8,128)(2,1)} %all-gather.3.cloned.1.call-done, bf16[1024,4096]{1,0:T(8,128)(2,1)} %all-gather.5.cloned.1.call-done, bf16[256,4096]{1,0:T(8,128)(2,1)S(1)} %copy-done, pred[1024,256]{1,0:T(8,128)(4,1)S(1)} %compare_reduce_fusion, f32[1024,256]{1,0:T(8,128)S(1)} %copy-done.3), kind=kOutput, calls=%fused_computation.1 | convolution fusion | flops 4300210176 | bytes 24379392 | tf_op jit(solution)/shard_map/dot_general | solution.py:150
  313.5 0.0 reduce-scatter.6.cloned.1.call-update
  313.5 32.4 %reduce-scatter.8.cloned.1.call-done = f32[1024,256]{1,0:T(8,128)} async-done(((f32[4096,256]{1,0:T(8,128)}), f32[1024,256]{1,0:T(8,128)}) %reduce-scatter.8.cloned.1.call-update) | async-done | bytes 1048592 | tf_op jit(solution)/shard_map/reduce_scatter | solution.py:156
  345.9 2.1 convert_element_type.53
  348.0 53.8 %reduce-scatter.6.cloned.1.call-done = f32[1024,256]{1,0:T(8,128)} async-done(((f32[4096,256]{1,0:T(8,128)}), f32[1024,256]{1,0:T(8,128)}) %reduce-scatter.6.cloned.1.call-update) | async-done | bytes 1048592 | tf_op jit(solution)/shard_map/reduce_scatter | solution.py:156
  401.7 2.1 convert_element_type.52
  (10 shorter events, 0.0 us)
Async XLA Ops:
  7.2 101.6 %copy-start = (bf16[256,4096]{1,0:T(8,128)(2,1)S(1)}, bf16[256,4096]{1,0:T(8,128)(2,1)}, u32[]{:S(2)}) copy-start(bf16[256,4096]{1,0:T(8,128)(2,1)} %param.10) | copy-start | bytes 6291460
  7.2 91.0 %all-gather.3.cloned.1.call-start = ((), (), s32[]{:S(2)}) async-start(), calls=%async_computation.3 | async-start | bytes 9732096 | tf_op jit(solution)/shard_map/all_gather | solution.py:123
  9.6 90.6 %copy-start.5 = (f32[256]{0:T(256)S(1)}, f32[256]{0:T(256)}, u32[]{:S(2)}) copy-start(f32[256]{0:T(256)} %param.9) | copy-start | bytes 3076
  11.1 191.7 %reduce-scatter.4.cloned.1.call-start = ((), (), s32[]{:S(2)}) async-start(), calls=%async_computation.4 | async-start | bytes 9437184 | tf_op jit(solution)/shard_map/reduce_scatter | solution.py:137
  107.7 1.0 copy-start.2
  114.5 88.3 %copy-start.1 = (bf16[128,4096]{1,0:T(8,128)(2,1)S(1)}, bf16[128,4096]{1,0:T(8,128)(2,1)}, u32[]{:S(2)}) copy-start(bf16[128,4096]{1,0:T(8,128)(2,1)} %param.6) | copy-start | bytes 3145732
  114.5 88.3 %copy-start.4 = (f32[4096]{0:T(1024)S(1)}, f32[4096]{0:T(1024)}, u32[]{:S(2)}) copy-start(f32[4096]{0:T(1024)} %param.11) | copy-start | bytes 49156
  114.5 171.8 %all-gather.5.cloned.1.call-start = ((), (), s32[]{:S(2)}) async-start(), calls=%async_computation.5 | async-start | bytes 9437184 | tf_op jit(solution)/shard_map/all_gather | solution.py:143
  205.8 140.1 %reduce-scatter.8.cloned.1.call-start = ((), (), s32[]{:S(2)}) async-start(), calls=%async_computation.7 | async-start | bytes 5242880 | tf_op jit(solution)/shard_map/reduce_scatter | solution.py:156
  294.5 1.2 copy-start.3
  294.5 107.2 %reduce-scatter.6.cloned.1.call-start = ((), (), s32[]{:S(2)}) async-start(), calls=%async_computation.6 | async-start | bytes 5242880 | tf_op jit(solution)/shard_map/reduce_scatter | solution.py:156
Sparse Core Ops, SparseCore 0:
  11.2 86.9 all-gather.2
  114.6 88.1 reduce-scatter.3
  205.9 80.3 all-gather.4
  294.7 51.2 reduce-scatter.7
  349.0 52.6 reduce-scatter.5
